TPU v7x, 32 devices: a whole 2x2x4 slice. The times are simulated.
32 devices in a mesh: dp: 8 (over y, x, core), fsdp: 4 (over z).
Axes of the slice: x: 2, y: 2, z: 4, core: 2. Of those that a mesh axis runs over, the one named last changes fastest.
Arguments:
- tokens: bfloat16 [32768, 768], P(('dp', 'fsdp')), may hold values from -6 to 6
- cotangent: bfloat16 [32768, 768], P(('dp', 'fsdp')), may hold values from -6 to 6
- doc_lengths: int32 [64, 4], P(('dp', 'fsdp')), may hold values from 1 to 288, 512 in all within a row
- query_ids: int32 [256, 1], P(('dp', 'fsdp')), may hold values from 0 to 63
- qkv_weight: bfloat16 [768, 2304], P(('dp', 'fsdp')), may hold values from -0.21875 to 0.21875
- query_bias: bfloat16 [768], P(('dp', 'fsdp')), may hold values from -3 to 3
- value_bias: bfloat16 [768], P(('dp', 'fsdp')), may hold values from -3 to 3
- attn_weight: bfloat16 [768, 768], P(('dp', 'fsdp')), may hold values from -0.875 to 0.875
- attn_bias: bfloat16 [768], P(('dp', 'fsdp')), may hold values from -2 to 2
- first_gain: bfloat16 [768], P(('dp', 'fsdp')), may hold values from 0.5 to 1.5
- first_shift: bfloat16 [768], P(('dp', 'fsdp')), may hold values from -2 to 2
- inner_weight: bfloat16 [768, 3072], P(('dp', 'fsdp')), may hold values from -0.21875 to 0.21875
- inner_bias: bfloat16 [3072], P(('dp', 'fsdp')), may hold values from -3 to 3
- outer_weight: bfloat16 [3072, 768], P(('dp', 'fsdp')), may hold values from -0.21875 to 0.21875
- outer_bias: bfloat16 [768], P(('dp', 'fsdp')), may hold values from -2 to 2
- second_gain: bfloat16 [768], P(('dp', 'fsdp')), may hold values from 0.5 to 1.5
- second_shift: bfloat16 [768], P(('dp', 'fsdp')), may hold values from -2 to 2
- span_weight: bfloat16 [768, 128], P(('dp', 'fsdp')), may hold values from -0.21875 to 0.21875
- answer_vector: bfloat16 [128], P(('dp', 'fsdp')), may hold values from -1 to 1
Outputs:
- log_likelihood: float32 [], replicated
- layer_output: bfloat16 [32768, 768], P(('dp', 'fsdp'))
- input_grad: float32 [32768, 768], P(('dp', 'fsdp'))
- qkv_weight_grad: float32 [768, 2304], P(('dp', 'fsdp'))
- query_bias_grad: float32 [768], P(('dp', 'fsdp'))
- value_bias_grad: float32 [768], P(('dp', 'fsdp'))
- attn_weight_grad: float32 [768, 768], P(('dp', 'fsdp'))
- attn_bias_grad: float32 [768], P(('dp', 'fsdp'))
- first_gain_grad: float32 [768], P(('dp', 'fsdp'))
- first_shift_grad: float32 [768], P(('dp', 'fsdp'))
- inner_weight_grad: float32 [768, 3072], P(('dp', 'fsdp'))
- inner_bias_grad: float32 [3072], P(('dp', 'fsdp'))
- outer_weight_grad: float32 [3072, 768], P(('dp', 'fsdp'))
- outer_bias_grad: float32 [768], P(('dp', 'fsdp'))
- second_gain_grad: float32 [768], P(('dp', 'fsdp'))
- second_shift_grad: float32 [768], P(('dp', 'fsdp'))
- span_weight_grad: float32 [768, 128], P(('dp', 'fsdp'))
- answer_vector_grad: float32 [128], P(('dp', 'fsdp'))
Inputs may be any that keep to these rules, and one draw needn't show every extreme that they name: `doc_lengths`: the 4 lengths of a pack sum to 512, and in every pack one of them is 288. `query_ids`: every query has one segment or more.
All inputs are finite; a program needn't handle non-finite values.
Results may differ from a plain program's by a relative error of at most 0.014.
Values may be sent and summed in bfloat16 or wider, within the bound.
No kernel may reach another device: no remote copies, remote signals or barrier semaphores. Data moves between devices by JAX's collectives and lax.ppermute only.
A program may use at most 192 MiB of HBM per device.

v0:
```python
import math
import jax
import jax.numpy as jnp
from jax import lax
from jax.sharding import PartitionSpec as P

HEADS = 12
HEAD_DIM = 64
PACK = 512
SEGS_PACK = 4
HIGHEST = lax.Precision.HIGHEST
MASKED = -1e30


def matmul(operand, matrix):
    return jnp.dot(operand, matrix, preferred_element_type=jnp.float32)


def weight_grad(operand, matrix):
    return lax.dot_general(
        operand, matrix, (((0,), (0,)), ((), ())), preferred_element_type=jnp.float32
    )


def back_prod(operand, matrix):
    return lax.dot_general(
        operand, matrix, (((1,), (1,)), ((), ())), preferred_element_type=jnp.float32
    )


def normalize(hidden):
    center = hidden - jnp.mean(hidden, axis=-1, keepdims=True)
    factor = lax.rsqrt(jnp.mean(center * center, axis=-1, keepdims=True) + 1e-06)
    return (center * factor, factor)


def norm_back(gradient, normed, factor):
    return factor * (
        gradient
        - jnp.mean(gradient, axis=-1, keepdims=True)
        - normed * jnp.mean(gradient * normed, axis=-1, keepdims=True)
    )


def segment_ids(lengths):
    bounds = jnp.cumsum(lengths, axis=1)
    places = lax.broadcasted_iota(jnp.int32, (1, PACK, 1), 1)
    return jnp.sum((places >= bounds[:, None, :]).astype(jnp.int32), axis=-1)


def exact_gelu(inner_pre):
    return jax.nn.gelu(inner_pre, approximate=False)


def masked_scores(query_heads, key_heads, segment):
    scaling = 1.0 / math.sqrt(query_heads.shape[-1])
    same_segment = segment[:, None] == segment[None, :]
    raw_scores = (
        jnp.einsum("qhd,khd->hqk", query_heads, key_heads, preferred_element_type=jnp.float32)
        * scaling
    )
    return jnp.where(same_segment[None], raw_scores, MASKED)


def attend(pieces):
    query_heads, key_heads, value_heads, segment = pieces
    scores = masked_scores(query_heads, key_heads, segment)
    highest = jnp.max(scores, axis=-1, keepdims=True)
    weights = jnp.exp(scores - highest)
    totals = jnp.sum(weights, axis=-1, keepdims=True)
    shares = (weights / totals).astype(jnp.bfloat16)
    context = jnp.einsum("hqk,khd->qhd", shares, value_heads, preferred_element_type=jnp.float32)
    return (context.astype(jnp.bfloat16), highest + jnp.log(totals))


def attend_back(pieces):
    query_heads, key_heads, value_heads, segment, logsum, context_grad = pieces
    scaling = 1.0 / math.sqrt(query_heads.shape[-1])
    scores = masked_scores(query_heads, key_heads, segment)
    softmax = jnp.exp(scores - logsum)
    value_grad = jnp.einsum(
        "hqk,qhd->khd",
        softmax.astype(jnp.bfloat16),
        context_grad,
        preferred_element_type=jnp.float32,
    )
    shares_grad = jnp.einsum(
        "qhd,khd->hqk", context_grad, value_heads, preferred_element_type=jnp.float32
    )
    score_grad = softmax * (shares_grad - jnp.sum(softmax * shares_grad, axis=-1, keepdims=True))
    score_low = score_grad.astype(jnp.bfloat16)
    query_grad = (
        jnp.einsum("hqk,khd->qhd", score_low, key_heads, preferred_element_type=jnp.float32)
        * scaling
    )
    key_grad = (
        jnp.einsum("hqk,qhd->khd", score_low, query_heads, preferred_element_type=jnp.float32)
        * scaling
    )
    stacked = jnp.stack([query_grad, key_grad, value_grad], axis=1)
    return stacked.reshape(stacked.shape[0], -1)


def shards(
    tokens,
    cotangent,
    doc_lengths,
    query_ids,
    qkv_weight,
    query_bias,
    value_bias,
    attn_weight,
    attn_bias,
    first_gain,
    first_shift,
    inner_weight,
    inner_bias,
    outer_weight,
    outer_bias,
    second_gain,
    second_shift,
    span_weight,
    answer_vector,
):
    rows_here = tokens.shape[0]
    width = tokens.shape[1]
    packs_here = rows_here // PACK
    gathered = (
        lax.all_gather(qkv_weight, ("dp", "fsdp"), axis=0, tiled=True),
        lax.all_gather(query_bias, ("dp", "fsdp"), axis=0, tiled=True),
        lax.all_gather(value_bias, ("dp", "fsdp"), axis=0, tiled=True),
        lax.all_gather(attn_weight, ("dp", "fsdp"), axis=0, tiled=True),
        lax.all_gather(attn_bias, ("dp", "fsdp"), axis=0, tiled=True),
        lax.all_gather(first_gain, ("dp", "fsdp"), axis=0, tiled=True),
        lax.all_gather(first_shift, ("dp", "fsdp"), axis=0, tiled=True),
        lax.all_gather(inner_weight, ("dp", "fsdp"), axis=0, tiled=True),
        lax.all_gather(inner_bias, ("dp", "fsdp"), axis=0, tiled=True),
        lax.all_gather(outer_weight, ("dp", "fsdp"), axis=0, tiled=True),
        lax.all_gather(outer_bias, ("dp", "fsdp"), axis=0, tiled=True),
        lax.all_gather(second_gain, ("dp", "fsdp"), axis=0, tiled=True),
        lax.all_gather(second_shift, ("dp", "fsdp"), axis=0, tiled=True),
        lax.all_gather(span_weight, ("dp", "fsdp"), axis=0, tiled=True),
        lax.all_gather(answer_vector, ("dp", "fsdp"), axis=0, tiled=True),
    )
    (
        mix_full,
        query_add,
        value_add,
        attn_full,
        attn_add,
        gain_one,
        shift_one,
        inner_full,
        inner_add,
        outer_full,
        outer_add,
        gain_two,
        shift_two,
        span_full,
        answer_full,
    ) = gathered
    segment = segment_ids(doc_lengths)
    qkv_add = jnp.concatenate([query_add, jnp.zeros_like(query_add), value_add]).astype(jnp.float32)
    mixed_rows = (matmul(tokens, mix_full) + qkv_add).astype(jnp.bfloat16)
    head_split = mixed_rows.reshape(packs_here, PACK, 3, HEADS, HEAD_DIM)
    query_heads = head_split[:, :, 0]
    key_heads = head_split[:, :, 1]
    value_heads = head_split[:, :, 2]
    context, logsum = lax.map(attend, (query_heads, key_heads, value_heads, segment))
    context = context.reshape(rows_here, width)
    attended = matmul(context, attn_full) + attn_add.astype(jnp.float32)
    normed_one, factor_one = normalize(tokens.astype(jnp.float32) + attended)
    first_norm = normed_one * gain_one.astype(jnp.float32) + shift_one.astype(jnp.float32)
    first_low = first_norm.astype(jnp.bfloat16)
    inner_pre = matmul(first_low, inner_full) + inner_add.astype(jnp.float32)
    active, gelu_back = jax.vjp(exact_gelu, inner_pre)
    active_low = active.astype(jnp.bfloat16)
    outer_out = matmul(active_low, outer_full) + outer_add.astype(jnp.float32)
    normed_two, factor_two = normalize(first_norm + outer_out)
    result = (normed_two * gain_two.astype(jnp.float32) + shift_two.astype(jnp.float32)).astype(
        jnp.bfloat16
    )
    span_rows = matmul(result, span_full)
    answer_wide = answer_full.astype(jnp.float32)
    token_score = jnp.dot(span_rows, answer_wide, precision=HIGHEST).reshape(packs_here, PACK)
    member = segment[:, None, :] == lax.broadcasted_iota(jnp.int32, (1, SEGS_PACK, 1), 1)
    doc_score = jax.nn.logsumexp(jnp.where(member, token_score[:, None, :], MASKED), axis=-1)
    doc_flat = doc_score.reshape(-1)
    queries_all = packs_here * lax.axis_size("dp") * lax.axis_size("fsdp")
    member_query = query_ids == lax.broadcasted_iota(jnp.int32, (1, queries_all), 1)
    local_peak = jnp.max(jnp.where(member_query, doc_flat[:, None], MASKED), axis=0)
    local_mass = jnp.sum(
        jnp.where(member_query, jnp.exp(doc_flat[:, None] - local_peak[None, :]), 0.0), axis=0
    )
    peak_score = lax.pmax(local_peak, ("dp", "fsdp"))
    mass_total = lax.psum(local_mass * jnp.exp(local_peak - peak_score), ("dp", "fsdp"))
    marginal = peak_score + jnp.log(mass_total)
    likelihood = jnp.sum(marginal)
    gathered = (
        lax.all_gather(qkv_weight, ("dp", "fsdp"), axis=0, tiled=True),
        lax.all_gather(query_bias, ("dp", "fsdp"), axis=0, tiled=True),
        lax.all_gather(value_bias, ("dp", "fsdp"), axis=0, tiled=True),
        lax.all_gather(attn_weight, ("dp", "fsdp"), axis=0, tiled=True),
        lax.all_gather(attn_bias, ("dp", "fsdp"), axis=0, tiled=True),
        lax.all_gather(first_gain, ("dp", "fsdp"), axis=0, tiled=True),
        lax.all_gather(first_shift, ("dp", "fsdp"), axis=0, tiled=True),
        lax.all_gather(inner_weight, ("dp", "fsdp"), axis=0, tiled=True),
        lax.all_gather(inner_bias, ("dp", "fsdp"), axis=0, tiled=True),
        lax.all_gather(outer_weight, ("dp", "fsdp"), axis=0, tiled=True),
        lax.all_gather(outer_bias, ("dp", "fsdp"), axis=0, tiled=True),
        lax.all_gather(second_gain, ("dp", "fsdp"), axis=0, tiled=True),
        lax.all_gather(second_shift, ("dp", "fsdp"), axis=0, tiled=True),
        lax.all_gather(span_weight, ("dp", "fsdp"), axis=0, tiled=True),
        lax.all_gather(answer_vector, ("dp", "fsdp"), axis=0, tiled=True),
    )
    (
        mix_full,
        query_add,
        value_add,
        attn_full,
        attn_add,
        gain_one,
        shift_one,
        inner_full,
        inner_add,
        outer_full,
        outer_add,
        gain_two,
        shift_two,
        span_full,
        answer_full,
    ) = gathered
    seg_marginal = jnp.sum(jnp.where(member_query, marginal[None, :], 0.0), axis=1).reshape(
        packs_here, SEGS_PACK
    )
    doc_weight = jnp.exp(doc_score - seg_marginal)
    token_weight = jnp.sum(
        jnp.where(
            member,
            doc_weight[:, :, None] * jnp.exp(token_score[:, None, :] - doc_score[:, :, None]),
            0.0,
        ),
        axis=1,
    ).reshape(rows_here)
    answer_grad = jnp.dot(token_weight, span_rows, precision=HIGHEST)
    span_grad = (token_weight[:, None] * answer_full.astype(jnp.float32)[None, :]).astype(
        jnp.bfloat16
    )
    span_weight_grad = weight_grad(result, span_grad)
    result_grad = cotangent.astype(jnp.float32) + back_prod(span_grad, span_full)
    second_gain_grad = jnp.sum(result_grad * normed_two, axis=0)
    second_shift_grad = jnp.sum(result_grad, axis=0)
    second_sum_grad = norm_back(result_grad * gain_two.astype(jnp.float32), normed_two, factor_two)
    outer_low = second_sum_grad.astype(jnp.bfloat16)
    outer_weight_grad = weight_grad(active_low, outer_low)
    outer_bias_grad = jnp.sum(outer_low.astype(jnp.float32), axis=0)
    (inner_grad,) = gelu_back(back_prod(outer_low, outer_full))
    inner_low = inner_grad.astype(jnp.bfloat16)
    inner_weight_grad = weight_grad(first_low, inner_low)
    inner_bias_grad = jnp.sum(inner_low.astype(jnp.float32), axis=0)
    first_grad = second_sum_grad + back_prod(inner_low, inner_full)
    first_gain_grad = jnp.sum(first_grad * normed_one, axis=0)
    first_shift_grad = jnp.sum(first_grad, axis=0)
    first_sum_grad = norm_back(first_grad * gain_one.astype(jnp.float32), normed_one, factor_one)
    attended_low = first_sum_grad.astype(jnp.bfloat16)
    attn_weight_grad = weight_grad(context, attended_low)
    attn_bias_grad = jnp.sum(attended_low.astype(jnp.float32), axis=0)
    context_grad = back_prod(attended_low, attn_full).astype(jnp.bfloat16)
    context_grad = context_grad.reshape(packs_here, PACK, HEADS, HEAD_DIM)
    mixed_grad = lax.map(
        attend_back, (query_heads, key_heads, value_heads, segment, logsum, context_grad)
    )
    mixed_low = mixed_grad.reshape(rows_here, 3 * width).astype(jnp.bfloat16)
    qkv_weight_grad = weight_grad(tokens, mixed_low)
    bias_sums = jnp.sum(mixed_low.astype(jnp.float32), axis=0)
    query_bias_grad = bias_sums[:width]
    value_bias_grad = bias_sums[2 * width :]
    input_grad = back_prod(mixed_low, mix_full) + first_sum_grad
    owned_grads = (
        lax.psum_scatter(qkv_weight_grad, ("dp", "fsdp"), scatter_dimension=0, tiled=True),
        lax.psum_scatter(query_bias_grad, ("dp", "fsdp"), scatter_dimension=0, tiled=True),
        lax.psum_scatter(value_bias_grad, ("dp", "fsdp"), scatter_dimension=0, tiled=True),
        lax.psum_scatter(attn_weight_grad, ("dp", "fsdp"), scatter_dimension=0, tiled=True),
        lax.psum_scatter(attn_bias_grad, ("dp", "fsdp"), scatter_dimension=0, tiled=True),
        lax.psum_scatter(first_gain_grad, ("dp", "fsdp"), scatter_dimension=0, tiled=True),
        lax.psum_scatter(first_shift_grad, ("dp", "fsdp"), scatter_dimension=0, tiled=True),
        lax.psum_scatter(inner_weight_grad, ("dp", "fsdp"), scatter_dimension=0, tiled=True),
        lax.psum_scatter(inner_bias_grad, ("dp", "fsdp"), scatter_dimension=0, tiled=True),
        lax.psum_scatter(outer_weight_grad, ("dp", "fsdp"), scatter_dimension=0, tiled=True),
        lax.psum_scatter(outer_bias_grad, ("dp", "fsdp"), scatter_dimension=0, tiled=True),
        lax.psum_scatter(second_gain_grad, ("dp", "fsdp"), scatter_dimension=0, tiled=True),
        lax.psum_scatter(second_shift_grad, ("dp", "fsdp"), scatter_dimension=0, tiled=True),
        lax.psum_scatter(span_weight_grad, ("dp", "fsdp"), scatter_dimension=0, tiled=True),
        lax.psum_scatter(answer_grad, ("dp", "fsdp"), scatter_dimension=0, tiled=True),
    )
    return (likelihood, result, input_grad) + tuple(owned_grads)


def solution(mesh):
    in_specs = (
        P(("dp", "fsdp"), None),
        P(("dp", "fsdp"), None),
        P(("dp", "fsdp"), None),
        P(("dp", "fsdp"), None),
        P(("dp", "fsdp"), None),
        P(("dp", "fsdp")),
        P(("dp", "fsdp")),
        P(("dp", "fsdp"), None),
        P(("dp", "fsdp")),
        P(("dp", "fsdp")),
        P(("dp", "fsdp")),
        P(("dp", "fsdp"), None),
        P(("dp", "fsdp")),
        P(("dp", "fsdp"), None),
        P(("dp", "fsdp")),
        P(("dp", "fsdp")),
        P(("dp", "fsdp")),
        P(("dp", "fsdp"), None),
        P(("dp", "fsdp")),
    )
    out_specs = (
        P(),
        P(("dp", "fsdp"), None),
        P(("dp", "fsdp"), None),
        P(("dp", "fsdp"), None),
        P(("dp", "fsdp")),
        P(("dp", "fsdp")),
        P(("dp", "fsdp"), None),
        P(("dp", "fsdp")),
        P(("dp", "fsdp")),
        P(("dp", "fsdp")),
        P(("dp", "fsdp"), None),
        P(("dp", "fsdp")),
        P(("dp", "fsdp"), None),
        P(("dp", "fsdp")),
        P(("dp", "fsdp")),
        P(("dp", "fsdp")),
        P(("dp", "fsdp"), None),
        P(("dp", "fsdp")),
    )
    return jax.shard_map(shards, mesh=mesh, in_specs=in_specs, out_specs=out_specs, check_vma=False)
```

profile of v0, /device:TPU:0, one launch (start us, length us, event | category | flops | bytes accessed | tf_op | source)
XLA Modules:
  0.0 978.1 jit_solution(9499859527295209149)
XLA Ops:
  19.5 42.6 %all-reduce.22 = (bf16[768]{0:T(1024)(128)(2,1)S(1)}, bf16[768]{0:T(1024)(128)(2,1)S(1)}, bf16[768]{0:T(1024)(128)(2,1)S(1)}, bf16[768]{0:T(1024)(128)(2,1)S(1)}...) all-reduce(bf16[768]{0:T(1024)(128)(2,1)S(1)} %dynamic-update-slice, ...), channel_id=1, replica_groups=mesh['dp'=8,'fsdp'=4] {'dp','fsdp'}, use_global_device_ids=true, to_apply=%add.1 | all-reduce | flops 9344 | bytes 37376
  62.1 2.6 copy.106
  66.5 72.9 %all_gather.66 = bf16[768,128]{1,0:T(8,128)(2,1)} all-gather(bf16[24,128]{1,0:T(8,128)(2,1)S(1)} %copy-done.34), channel_id=1, replica_groups=mesh['dp'=8,'fsdp'=4] {'dp','fsdp'}, dimensions={0}, use_global_device_ids=true | all-gather | bytes 202752 | tf_op jit(solution)/shard_map/all_gather | solution.py:142
  139.9 1.6 copy.113
  141.6 7.5 add_convert_fusion.1
  149.1 6.6 copy.107
  155.7 8.9 reshape.253
  164.6 5.4 slice_bitcast_fusion
  172.1 20.9 %while.22 = (s32[]{:T(128)}, bf16[2,512,12,64]{1,3,2,0:T(8,128)(2,1)}, f32[2,12,512,1]{2,1,3,0:T(8,128)S(1)}, bf16[2,512,12,64]{1,3,2,0:T(8,128)(2,1)}, s32[2,51...) while((s32[]{:T(128)}, ...), condition=%wide.region_5.6_spmd, body=%wide.region_2.5_spmd.sunk | while | flops 843704320 | bytes 42172508 | solution.py:169
  172.3 2.1 fusion.124
  174.4 2.6 fusion.125
  177.0 5.5 fusion.126
  182.7 2.1 fusion.124
  184.8 2.6 fusion.125
  187.3 5.5 fusion.126
  193.0 4.2 copy.111
  197.2 1.6 copy.159
  198.8 3.9 fusion.79
  202.7 1.6 copy-done.9
  204.8 37.9 %multiply_convert_fusion.1 = (bf16[1024,3072]{1,0:T(8,128)(2,1)}, f32[1024,3072]{1,0:T(8,128)}, f32[1024,3072]{1,0:T(8,128)}) fusion(f32[3072]{0:T(1024)S(1)} %convert_element_type.113, bf16[768,3072]{1,0:T(8,128)(2,1)} %all-gather.9.cloned.1.call-done, f32[1024,768]{0,1:T(8,128)} %copy-done.9, f32[768]{0:T(1024)S(1)} %convert_element_type.111, ...), kind=kOutput, calls=%fused_computation.64 | convolution fusion | flops 5043388416 | bytes 39348224 | tf_op jit(solution)/shard_map/dot_general | solution.py:16
  242.7 17.4 %all-gather.11.cloned.1.call-done = bf16[3072,768]{1,0:T(8,128)(2,1)} async-done(((bf16[96,768]{1,0:T(8,128)(2,1)}), bf16[3072,768]{1,0:T(8,128)(2,1)}) %all-gather.11.cloned.1.call-update) | async-done | bytes 4718608 | tf_op jit(solution)/shard_map/all_gather | solution.py:138
  260.2 9.7 fusion.80
  270.3 1.7 add_convert_fusion.2
  272.0 2.0 fusion.81
  275.8 39.6 %pmax.7 = f32[64]{0:T(128)S(1)} all-reduce(f32[64]{0:T(128)S(1)} %select_reduce_fusion.4), channel_id=1, replica_groups=mesh['dp'=8,'fsdp'=4] {'dp','fsdp'}, use_global_device_ids=true, to_apply=%region_13.14 | all-reduce | flops 64 | bytes 512 | tf_op jit(solution)/shard_map/pmax | solution.py:195
  315.5 39.5 %psum.7 = f32[64]{0:T(128)S(1)} all-reduce(f32[64]{0:T(128)S(1)} %exponential_multiply_fusion), channel_id=1, replica_groups=mesh['dp'=8,'fsdp'=4] {'dp','fsdp'}, use_global_device_ids=true, to_apply=%region_15.16 | all-reduce | flops 64 | bytes 512 | tf_op jit(solution)/shard_map/psum | solution.py:196
  356.0 2.9 fusion.54
  358.9 5.1 multiply_reduce_fusion.1
  364.0 5.2 convert_reduce_fusion.2
  369.2 20.2 %convert_reduce_fusion = (f32[3072]{0:T(1024)}, bf16[1024,3072]{1,0:T(8,128)(2,1)}) fusion(f32[1024,3072]{1,0:T(8,128)} %get-tuple-element.293, bf16[3072,768]{1,0:T(8,128)(2,1)} %all-gather.11.cloned.1.call-done, f32[1024,768]{0,1:T(8,128)} %get-tuple-element.285, f32[1024,3072]{1,0:T(8,128)} %get-tuple-element.305, f32[3072]{0:T(1024)S(1)} %convert_element_type.113), kind=kOutput, calls=%fused_computation.62 | convolution fusion | flops 4886098944 | bytes 39346176 | tf_op jit(solution)/shard_map/dot_general | solution.py:26
  389.4 10.8 %multiply_reduce_fusion.2 = (f32[768]{0:T(1024)}, f32[1024]{0:T(1024)S(1)}, f32[1024]{0:T(1024)S(1)}, f32[768]{0:T(1024)}, f32[1024,768]{0,1:T(8,128)S(1)}) fusion(f32[1024,768]{0,1:T(8,128)S(1)} %copy-done.10, f32[1024]{0:T(1024)S(1)} %add_rsqrt_fusion.1, f32[1024]{0:T(1024)S(1)} %broadcast_multiply_fusion.5, f32[768]{0:T(1024)S(1)} %convert_element_type.110, ...), kind=kOutput, calls=%fused_computation.83 | convolution fusion | flops 4839698432 | bytes 20472832 | tf_op jit(solution)/shard_map/dot_general | solution.py:26
  400.2 1.7 convert_reduce_fusion.3
  401.9 1.6 copy-done.14
  407.1 1.5 copy.119
  408.6 5.4 fusion.64
  414.1 57.4 %while.23 = (s32[]{:T(128)}, bf16[2,512,2304]{2,1,0:T(8,128)(2,1)}, bf16[2,512,12,64]{1,3,2,0:T(8,128)(2,1)S(1)}, s32[2,512]{1,0:T(2,128)S(1)}, bf16[2,512,12,64...) while((s32[]{:T(128)}, bf16[2,512,2304]{2,1,0:T(8,128)(2,1)}, ...), condition=%wide.region_25.26_spmd, body=%wide.region_23.25_spmd.sunk | while | flops 2064640000 | bytes 149095184 | solution.py:270
  414.1 1.8 fusion.135
  416.3 6.9 multiply_reduce_fusion.10
  423.2 7.0 multiply_convert_fusion.6
  431.3 2.0 multiply_bitcast_fusion.4
  433.3 3.2 fusion.136
  436.8 2.6 copy.163
  439.4 3.4 constant_dynamic-update-slice_fusion.2
  442.7 1.8 fusion.135
  444.9 6.9 multiply_reduce_fusion.10
  451.8 7.0 multiply_convert_fusion.6
  459.9 2.0 multiply_bitcast_fusion.4
  461.9 3.2 fusion.136
  465.4 2.6 copy.163
  468.0 3.4 constant_dynamic-update-slice_fusion.2
  471.6 9.7 convolution_bitcast_fusion
  481.3 8.1 copy.134
  489.5 1.9 copy-done.15
  491.3 10.2 %fusion.67 = f32[3072,768]{1,0:T(8,128)} fusion(bf16[1024,3072]{1,0:T(8,128)(2,1)} %get-tuple-element.292, f32[1024,768]{0,1:T(8,128)S(1)} %copy-done.15), kind=kOutput, calls=%fused_computation.147 | convolution fusion | flops 4832624640 | bytes 18874368 | tf_op jit(solution)/shard_map/dot_general | solution.py:20
  501.7 1.8 copy-done.11
  503.5 10.5 %fusion.71 = f32[768,3072]{1,0:T(8,128)} fusion(bf16[1024,3072]{1,0:T(8,128)(2,1)} %get-tuple-element.311, f32[1024,768]{0,1:T(8,128)S(1)} %copy-done.11, f32[768]{0:T(1024)S(1)} %copy-done.40, f32[768]{0:T(1024)S(1)} %copy-done.29, f32[1024]{0:T(1024)S(1)} %copy-done.31, f32[1024]{0:T(1024)S(1)} %copy-done.22), kind=kOutput, calls=%fused_computation.151 | convolution fusion | flops 4835770368 | bytes 18888704 | tf_op jit(solution)/shard_map/dot_general | solution.py:20
  514.1 2.7 copy.123
  517.1 3.1 convert_reduce_fusion.1
  520.3 41.8 %all-reduce.21 = (f32[768]{0:T(1024)S(1)}, f32[768]{0:T(1024)S(1)}, f32[768]{0:T(1024)S(1)}, f32[768]{0:T(1024)S(1)}, f32[768]{0:T(1024)S(1)}, /*index=5*/f32[30...) all-reduce(f32[768]{0:T(1024)S(1)} %get-tuple-element.302, ...), channel_id=3, replica_groups=mesh['dp'=8,'fsdp'=4] {'dp','fsdp'}, use_global_device_ids=true, to_apply=%region_28.29.clone | all-reduce | flops 9344 | bytes 74752
  566.7 8.1 convolution_add_fusion.1
  574.9 2.4 copy.124
  578.4 109.4 %reduce-scatter.16.cloned.1.call-done = f32[24,2304]{1,0:T(8,128)} async-done(((f32[768,2304]{1,0:T(8,128)}), f32[24,2304]{1,0:T(8,128)}) %reduce-scatter.16.cloned.1.call-update) | async-done | bytes 221200
  687.9 142.5 %reduce-scatter.14.cloned.1.call-done = f32[96,768]{1,0:T(8,128)} async-done(((f32[3072,768]{1,0:T(8,128)}), f32[96,768]{1,0:T(8,128)}) %reduce-scatter.14.cloned.1.call-update) | async-done | bytes 294928 | tf_op jit(solution)/shard_map/reduce_scatter | solution.py:289
  830.3 141.0 %reduce-scatter.12.cloned.1.call-done = f32[24,3072]{1,0:T(8,128)} async-done(((f32[768,3072]{1,0:T(8,128)}), f32[24,3072]{1,0:T(8,128)}) %reduce-scatter.12.cloned.1.call-update) | async-done | bytes 294928 | tf_op jit(solution)/shard_map/reduce_scatter | solution.py:287
  (220 shorter events, 34.1 us)
Async XLA Ops:
  7.2 59.3 %copy-start.34 = (bf16[24,128]{1,0:T(8,128)(2,1)S(1)}, bf16[24,128]{1,0:T(8,128)(2,1)}, u32[]{:S(2)}) copy-start(bf16[24,128]{1,0:T(8,128)(2,1)} %param.40) | copy-start | bytes 18436
  7.2 132.7 %copy-start.16 = (bf16[1024,768]{1,0:T(8,128)(2,1)S(1)}, bf16[1024,768]{1,0:T(8,128)(2,1)}, u32[]{:S(2)}) copy-start(bf16[1024,768]{1,0:T(8,128)(2,1)} %param.24) | copy-start | bytes 4718596
  7.2 134.3 %all-gather.5.cloned.1.call-start = ((), (), s32[]{:S(2)}) async-start(), calls=%async_computation.5 | async-start | bytes 3649536 | tf_op jit(solution)/shard_map/all_gather | solution.py:129
  7.9 133.6 %copy-start.17 = (bf16[1024,768]{1,0:T(8,128)(2,1)S(1)}, bf16[1024,768]{1,0:T(8,128)(2,1)}, u32[]{:S(2)}) copy-start(bf16[1024,768]{1,0:T(8,128)(2,1)} %param.23) | copy-start | bytes 4718596
  8.0 190.8 %all-gather.7.cloned.1.call-start = ((), (), s32[]{:S(2)}) async-start(), calls=%async_computation.6 | async-start | bytes 1216512 | tf_op jit(solution)/shard_map/all_gather | solution.py:132
  8.7 196.1 %all-gather.9.cloned.1.call-start = ((), (), s32[]{:S(2)}) async-start(), calls=%async_computation.7 | async-start | bytes 4866048 | tf_op jit(solution)/shard_map/all_gather | solution.py:136
  9.4 250.7 %all-gather.11.cloned.1.call-start = ((), (), s32[]{:S(2)}) async-start(), calls=%async_computation.8 | async-start | bytes 4866048 | tf_op jit(solution)/shard_map/all_gather | solution.py:138
  10.0 568.4 %reduce-scatter.18.cloned.1.call-start = ((), (), s32[]{:S(2)}) async-start(), calls=%async_computation.13 | async-start | bytes 405504
  62.1 87.0 %copy-start.43 = (bf16[128]{0:T(256)(128)(2,1)}, bf16[128]{0:T(256)(128)(2,1)S(1)}, u32[]{:S(2)}) copy-start(bf16[128]{0:T(256)(128)(2,1)S(1)} %get-tuple-element.283) | copy-start | bytes 772
  64.6 335.5 %copy-start.28 = (f32[768]{0:T(1024)}, f32[768]{0:T(1024)S(1)}, u32[]{:S(2)}) copy-start(f32[768]{0:T(1024)S(1)} %convert_element_type.110) | copy-start | bytes 9220
  64.7 195.5 %copy-start.39 = (f32[768]{0:T(1024)}, f32[768]{0:T(1024)S(1)}, u32[]{:S(2)}) copy-start(f32[768]{0:T(1024)S(1)} %convert_element_type.111) | copy-start | bytes 9220
  193.0 9.7 copy-start
  193.0 9.7 copy-start.3
  193.0 9.7 copy-start.19
  202.7 1.7 copy-start.9
  202.7 197.4 %copy-start.21 = (f32[1024]{0:T(1024)}, f32[1024]{0:T(1024)S(1)}, u32[]{:S(2)}) copy-start(f32[1024]{0:T(1024)S(1)} %broadcast_multiply_fusion.5) | copy-start | bytes 12292
  204.8 195.4 %copy-start.30 = (f32[1024]{0:T(1024)}, f32[1024]{0:T(1024)S(1)}, u32[]{:S(2)}) copy-start(f32[1024]{0:T(1024)S(1)} %add_rsqrt_fusion.1) | copy-start | bytes 12292
  204.8 55.4 %copy-start.41 = (f32[768]{0:T(1024)S(1)}, f32[768]{0:T(1024)}, u32[]{:S(2)}) copy-start(f32[768]{0:T(1024)} %convert_element_type.115) | copy-start | bytes 9220
  260.2 10.1 %copy-start.23 = (f32[768]{0:T(1024)S(1)}, f32[768]{0:T(1024)}, u32[]{:S(2)}) copy-start(f32[768]{0:T(1024)} %convert_element_type.116) | copy-start | bytes 9220
  260.2 10.1 %copy-start.32 = (f32[768]{0:T(1024)S(1)}, f32[768]{0:T(1024)}, u32[]{:S(2)}) copy-start(f32[768]{0:T(1024)} %convert_element_type.117) | copy-start | bytes 9220
  269.9 2.2 copy-start.18
  270.3 4.6 copy-start.44
  270.3 5.4 copy-start.45
  270.3 85.7 %copy-start.42 = (f32[128]{0:T(128)S(1)}, f32[128]{0:T(128)}, u32[]{:S(2)}) copy-start(f32[128]{0:T(128)} %convert_element_type.120) | copy-start | bytes 1540
  274.0 0.8 copy-start.12
  356.0 8.0 copy-start.24
  364.0 214.5 %reduce-scatter.10.cloned.1.call-start = ((), (), s32[]{:S(2)}) async-start(), calls=%async_computation.9 | async-start | bytes 2433024 | tf_op jit(solution)/shard_map/reduce_scatter | solution.py:283
  369.2 20.2 %copy-start.10 = (f32[1024,768]{0,1:T(8,128)S(1)}, f32[1024,768]{0,1:T(8,128)}, u32[]{:S(2)}) copy-start(f32[1024,768]{0,1:T(8,128)} %copy-done.9) | copy-start | bytes 9437188
  400.2 3.4 copy-start.46
  401.9 1.6 copy-start.14
  408.6 5.4 copy-start.1
  408.6 5.5 copy-start.4
  408.6 5.5 copy-start.20
  414.0 273.8 %reduce-scatter.16.cloned.1.call-start = ((), (), s32[]{:S(2)}) async-start(), calls=%async_computation.12 | async-start | bytes 7299072
  414.1 2.1 copy-start.6
  414.1 2.1 copy-start.7
  431.3 2.0 copy-start.8
  439.4 3.4 copy-start.2
  439.4 3.4 copy-start.5
  442.7 2.1 copy-start.6
  442.7 2.1 copy-start.7
  459.9 2.0 copy-start.8
  468.0 3.4 copy-start.2
  468.0 3.4 copy-start.5
  489.4 1.9 copy-start.15
  489.4 340.9 %reduce-scatter.14.cloned.1.call-start = ((), (), s32[]{:S(2)}) async-start(), calls=%async_computation.11 | async-start | bytes 9732096 | tf_op jit(solution)/shard_map/reduce_scatter | solution.py:289
  501.6 1.9 copy-start.11
  501.6 1.9 copy-start.22
  501.6 1.9 copy-start.29
  501.6 1.9 copy-start.31
  501.6 1.9 copy-start.40
  501.6 469.7 %reduce-scatter.12.cloned.1.call-start = ((), (), s32[]{:S(2)}) async-start(), calls=%async_computation.10 | async-start | bytes 9732096 | tf_op jit(solution)/shard_map/reduce_scatter | solution.py:287
  514.0 2.8 copy-start.25
  514.0 2.8 copy-start.13
  514.0 6.2 copy-start.26
  514.0 6.2 copy-start.27
  514.0 6.2 copy-start.33
  514.0 6.2 copy-start.35
  514.0 6.2 copy-start.36
  514.1 6.2 copy-start.37
  514.1 6.2 copy-start.38
Sparse Core Ops, SparseCore 0:
  10.8 63.2 all-gather.4
  76.9 52.7 all-gather.6
  132.5 62.5 all-gather.8
  197.8 62.3 all-gather.10
  364.1 94.5 reduce-scatter.17
  465.3 98.1 reduce-scatter.9
  569.7 118.0 reduce-scatter.15
  695.3 134.9 reduce-scatter.13
  836.8 134.4 reduce-scatter.11
where the time goes:
time: 983 us; the launch traced here: 978 us
  waiting for transfers between devices  413 us (42%)
  blocking collectives  236 us (24%)
  matrix products  191 us (19%)
  local copies, waits for them, and re-layouts  84 us (9%)
  other arithmetic  37.7 us (4%)
  between operations  14.8 us (2%)
    reduce_scatter x1, waiting for transfers between devices, shards(): lax.psum_scatter(outer_weight_grad, ('dp', 'fsdp'), scatter_dimension=0,...  142 us
    reduce_scatter x1, waiting for transfers between devices, shards(): lax.psum_scatter(inner_weight_grad, ('dp', 'fsdp'), scatter_dimension=0,...  141 us
    unnamed x11, waiting for transfers between devices  112 us
    unnamed x2, blocking collectives  84.4 us
    all_gather x1, blocking collectives, shards(): lax.all_gather(span_weight, ('dp', 'fsdp'), axis=0, tiled=True)  72.9 us
    dot_general x5, matrix products, matmul(): return jnp.dot(operand, matrix, preferred_element_type=jnp.float32)  61 us
    dot_general x5, matrix products, back_prod(): lax.dot_general(operand, matrix, (((1,), (1,)), ((), ())), preferred_elem...  45.6 us
    unnamed x123, local copies, waits for them, and re-layouts  41 us
  transfers between devices with their start and end apart: 9, of which 4 were waited for; matrix products, arithmetic and copies ran while one was open for 29% of the time, Pallas kernels for 0%

commit v1 on v0

--- a/solution.py
+++ b/solution.py
@@ -193,7 +193,8 @@
         jnp.where(member_query, jnp.exp(doc_flat[:, None] - local_peak[None, :]), 0.0), axis=0
     )
     peak_score = lax.pmax(local_peak, ("dp", "fsdp"))
-    mass_total = lax.psum(local_mass * jnp.exp(local_peak - peak_score), ("dp", "fsdp"))
+    block_here = local_mass * jnp.exp(local_peak - peak_score)
+    mass_total = jax.lax.psum(jax.lax.psum(block_here, "fsdp"), "dp")
     marginal = peak_score + jnp.log(mass_total)
     likelihood = jnp.sum(marginal)
     gathered = (

time: 983 us -> 963 us (0.980)
  blocking collectives: 236 us -> 217 us
    psum x1 -> x2, blocking collectives: 39.5 us -> 22.1 us  [shards(): mass_total = jax.lax.psum(jax.lax.psum(block_here, 'fsdp'), 'dp')]
where the time goes in v1:
time: 963 us; the launch traced here: 959 us
  waiting for transfers between devices  414 us (43%)
  blocking collectives  217 us (23%)
  matrix products  191 us (20%)
  local copies, waits for them, and re-layouts  84 us (9%)
  other arithmetic  37.7 us (4%)
  between operations  14.8 us (2%)
    reduce_scatter x1, waiting for transfers between devices, shards(): lax.psum_scatter(outer_weight_grad, ('dp', 'fsdp'), scatter_dimension=0,...  142 us
    reduce_scatter x1, waiting for transfers between devices, shards(): lax.psum_scatter(inner_weight_grad, ('dp', 'fsdp'), scatter_dimension=0,...  141 us
    unnamed x11, waiting for transfers between devices  113 us
    unnamed x2, blocking collectives  82.2 us
    all_gather x1, blocking collectives, shards(): lax.all_gather(span_weight, ('dp', 'fsdp'), axis=0, tiled=True)  72.9 us
    dot_general x5, matrix products, matmul(): return jnp.dot(operand, matrix, preferred_element_type=jnp.float32)  61.2 us
    dot_general x5, matrix products, back_prod(): lax.dot_general(operand, matrix, (((1,), (1,)), ((), ())), preferred_elem...  45.2 us
    unnamed x123, local copies, waits for them, and re-layouts  41 us
  transfers between devices with their start and end apart: 9, of which 4 were waited for; matrix products, arithmetic and copies ran while one was open for 29% of the time, Pallas kernels for 0%

profile of v1, /device:TPU:0, one launch (start us, length us, event | category | flops | bytes accessed | tf_op | source)
XLA Modules:
  0.0 958.9 jit_solution(8825059581699110310)
XLA Ops:
  19.5 42.6 %all-reduce.22 = (bf16[768]{0:T(1024)(128)(2,1)S(1)}, bf16[768]{0:T(1024)(128)(2,1)S(1)}, bf16[768]{0:T(1024)(128)(2,1)S(1)}, bf16[768]{0:T(1024)(128)(2,1)S(1)}...) all-reduce(bf16[768]{0:T(1024)(128)(2,1)S(1)} %dynamic-update-slice, ...), channel_id=1, replica_groups=mesh['dp'=8,'fsdp'=4] {'dp','fsdp'}, use_global_device_ids=true, to_apply=%add.1 | all-reduce | flops 9344 | bytes 37376
  62.1 2.6 copy.106
  66.5 72.9 %all_gather.66 = bf16[768,128]{1,0:T(8,128)(2,1)} all-gather(bf16[24,128]{1,0:T(8,128)(2,1)S(1)} %copy-done.34), channel_id=1, replica_groups=mesh['dp'=8,'fsdp'=4] {'dp','fsdp'}, dimensions={0}, use_global_device_ids=true | all-gather | bytes 202752 | tf_op jit(solution)/shard_map/all_gather | solution.py:142
  139.9 1.6 copy.113
  141.6 7.5 add_convert_fusion.1
  149.1 6.6 copy.107
  155.7 8.9 reshape.253
  164.6 5.4 slice_bitcast_fusion
  172.1 20.9 %while.22 = (s32[]{:T(128)}, bf16[2,512,12,64]{1,3,2,0:T(8,128)(2,1)}, f32[2,12,512,1]{2,1,3,0:T(8,128)S(1)}, bf16[2,512,12,64]{1,3,2,0:T(8,128)(2,1)}, s32[2,51...) while((s32[]{:T(128)}, ...), condition=%wide.region_5.6_spmd, body=%wide.region_2.5_spmd.sunk | while | flops 843704320 | bytes 42172508 | solution.py:169
  172.3 2.1 fusion.124
  174.4 2.6 fusion.125
  177.0 5.5 fusion.126
  182.7 2.1 fusion.124
  184.8 2.6 fusion.125
  187.3 5.5 fusion.126
  193.0 4.2 copy.111
  197.2 1.6 copy.159
  198.8 3.9 fusion.79
  202.8 1.6 copy-done.9
  204.8 37.9 %multiply_convert_fusion.1 = (bf16[1024,3072]{1,0:T(8,128)(2,1)}, f32[1024,3072]{1,0:T(8,128)}, f32[1024,3072]{1,0:T(8,128)}) fusion(f32[3072]{0:T(1024)S(1)} %convert_element_type.113, bf16[768,3072]{1,0:T(8,128)(2,1)} %all-gather.9.cloned.1.call-done, f32[1024,768]{0,1:T(8,128)} %copy-done.9, f32[768]{0:T(1024)S(1)} %convert_element_type.111, ...), kind=kOutput, calls=%fused_computation.64 | convolution fusion | flops 5043388416 | bytes 39348224 | tf_op jit(solution)/shard_map/dot_general | solution.py:16
  242.7 17.4 %all-gather.11.cloned.1.call-done = bf16[3072,768]{1,0:T(8,128)(2,1)} async-done(((bf16[96,768]{1,0:T(8,128)(2,1)}), bf16[3072,768]{1,0:T(8,128)(2,1)}) %all-gather.11.cloned.1.call-update) | async-done | bytes 4718608 | tf_op jit(solution)/shard_map/all_gather | solution.py:138
  260.2 9.9 %fusion.80 = (f32[1024]{0:T(1024)S(1)}, f32[1024,768]{0,1:T(8,128)S(1)}) fusion(f32[768]{0:T(1024)S(1)} %copy-done.41, bf16[1024,3072]{1,0:T(8,128)(2,1)} %get-tuple-element.292, bf16[3072,768]{1,0:T(8,128)(2,1)} %all-gather.11.cloned.1.call-done, f32[768]{0:T(1024)S(1)} %convert_element_type.111, f32[768]{0:T(1024)S(1)} %convert_element_type.110, ...), kind=kOutput, calls=%fused_computation.156 | convolution fusion | flops 4837342208 | bytes 17323008 | tf_op jit(solution)/shard_map/dot_general | solution.py:16
  270.5 1.7 add_convert_fusion.2
  272.2 2.0 fusion.81
  276.0 39.6 %pmax.7 = f32[64]{0:T(128)S(1)} all-reduce(f32[64]{0:T(128)S(1)} %select_reduce_fusion.4), channel_id=1, replica_groups=mesh['dp'=8,'fsdp'=4] {'dp','fsdp'}, use_global_device_ids=true, to_apply=%region_13.14 | all-reduce | flops 64 | bytes 512 | tf_op jit(solution)/shard_map/pmax | solution.py:195
  315.6 10.1 %psum.14 = f32[64]{0:T(128)S(1)} all-reduce(f32[64]{0:T(128)S(1)} %exponential_multiply_fusion), channel_id=1, replica_groups=mesh['dp'=8,'fsdp'=4] {'fsdp'}, use_global_device_ids=true, to_apply=%region_15.16 | all-reduce | flops 64 | bytes 512 | tf_op jit(solution)/shard_map/psum | solution.py:197
  325.7 12.0 %psum.15 = f32[64]{0:T(128)S(1)} all-reduce(f32[64]{0:T(128)S(1)} %psum.14), channel_id=1, replica_groups=mesh['dp'=8,'fsdp'=4] {'dp'}, use_global_device_ids=true, to_apply=%region_16.17 | all-reduce | flops 64 | bytes 512 | tf_op jit(solution)/shard_map/psum | solution.py:197
  338.7 2.8 fusion.54
  341.6 5.1 multiply_reduce_fusion.1
  346.8 5.2 convert_reduce_fusion.2
  352.0 19.7 %convert_reduce_fusion = (f32[3072]{0:T(1024)}, bf16[1024,3072]{1,0:T(8,128)(2,1)}) fusion(f32[1024,3072]{1,0:T(8,128)} %get-tuple-element.293, bf16[3072,768]{1,0:T(8,128)(2,1)} %all-gather.11.cloned.1.call-done, f32[1024,768]{0,1:T(8,128)} %get-tuple-element.285, f32[1024,3072]{1,0:T(8,128)} %get-tuple-element.305, f32[3072]{0:T(1024)S(1)} %convert_element_type.113), kind=kOutput, calls=%fused_computation.62 | convolution fusion | flops 4886098944 | bytes 39346176 | tf_op jit(solution)/shard_map/dot_general | solution.py:26
  371.7 10.8 %multiply_reduce_fusion.2 = (f32[768]{0:T(1024)}, f32[1024]{0:T(1024)S(1)}, f32[1024]{0:T(1024)S(1)}, f32[768]{0:T(1024)}, f32[1024,768]{0,1:T(8,128)S(1)}) fusion(f32[1024,768]{0,1:T(8,128)S(1)} %copy-done.10, f32[1024]{0:T(1024)S(1)} %add_rsqrt_fusion.1, f32[1024]{0:T(1024)S(1)} %broadcast_multiply_fusion.5, f32[768]{0:T(1024)S(1)} %convert_element_type.110, ...), kind=kOutput, calls=%fused_computation.83 | convolution fusion | flops 4839698432 | bytes 20472832 | tf_op jit(solution)/shard_map/dot_general | solution.py:26
  382.5 1.7 convert_reduce_fusion.3
  384.2 1.6 copy-done.14
  390.9 5.4 fusion.64
  396.5 57.5 %while.23 = (s32[]{:T(128)}, bf16[2,512,2304]{2,1,0:T(8,128)(2,1)}, bf16[2,512,12,64]{1,3,2,0:T(8,128)(2,1)S(1)}, s32[2,512]{1,0:T(2,128)S(1)}, bf16[2,512,12,64...) while((s32[]{:T(128)}, bf16[2,512,2304]{2,1,0:T(8,128)(2,1)}, ...), condition=%wide.region_26.27_spmd, body=%wide.region_24.26_spmd.sunk | while | flops 2064640000 | bytes 149095184 | solution.py:271
  396.5 1.8 fusion.135
  398.6 6.9 multiply_reduce_fusion.10
  405.5 7.0 multiply_convert_fusion.6
  413.7 2.0 multiply_bitcast_fusion.4
  415.7 3.2 fusion.136
  419.2 2.6 copy.163
  421.7 3.4 constant_dynamic-update-slice_fusion.2
  425.1 1.8 fusion.135
  427.2 6.9 multiply_reduce_fusion.10
  434.1 7.0 multiply_convert_fusion.6
  442.3 2.0 multiply_bitcast_fusion.4
  444.3 3.2 fusion.136
  447.8 2.6 copy.163
  450.3 3.4 constant_dynamic-update-slice_fusion.2
  454.0 9.7 %convolution_bitcast_fusion = f32[768,2304]{0,1:T(8,128)} fusion(bf16[1024,2304]{1,0:T(8,128)(2,1)} %bitcast.163, bf16[1024,768]{1,0:T(8,128)(2,1)} %param.23), kind=kOutput, calls=%fused_computation.80 | convolution fusion | flops 3623878656 | bytes 13369344 | tf_op jit(solution)/shard_map/dot_general | solution.py:20
  463.7 8.1 copy.134
  471.9 1.9 copy-done.15
  473.7 10.2 %fusion.67 = f32[3072,768]{1,0:T(8,128)} fusion(bf16[1024,3072]{1,0:T(8,128)(2,1)} %get-tuple-element.292, f32[1024,768]{0,1:T(8,128)S(1)} %copy-done.15), kind=kOutput, calls=%fused_computation.147 | convolution fusion | flops 4832624640 | bytes 18874368 | tf_op jit(solution)/shard_map/dot_general | solution.py:20
  484.1 1.8 copy-done.11
  485.9 10.5 %fusion.71 = f32[768,3072]{1,0:T(8,128)} fusion(bf16[1024,3072]{1,0:T(8,128)(2,1)} %get-tuple-element.311, f32[1024,768]{0,1:T(8,128)S(1)} %copy-done.11, f32[768]{0:T(1024)S(1)} %copy-done.40, f32[768]{0:T(1024)S(1)} %copy-done.29, f32[1024]{0:T(1024)S(1)} %copy-done.31, f32[1024]{0:T(1024)S(1)} %copy-done.22), kind=kOutput, calls=%fused_computation.151 | convolution fusion | flops 4835770368 | bytes 18888704 | tf_op jit(solution)/shard_map/dot_general | solution.py:20
  496.4 2.7 copy.123
  499.5 3.1 convert_reduce_fusion.1
  502.6 39.6 %all-reduce.21 = (f32[768]{0:T(1024)S(1)}, f32[768]{0:T(1024)S(1)}, f32[768]{0:T(1024)S(1)}, f32[768]{0:T(1024)S(1)}, f32[768]{0:T(1024)S(1)}, /*index=5*/f32[30...) all-reduce(f32[768]{0:T(1024)S(1)} %get-tuple-element.302, ...), channel_id=3, replica_groups=mesh['dp'=8,'fsdp'=4] {'dp','fsdp'}, use_global_device_ids=true, to_apply=%region_29.30.clone | all-reduce | flops 9344 | bytes 74752
  546.9 8.1 convolution_add_fusion.1
  555.0 2.4 copy.124
  558.5 110.1 %reduce-scatter.16.cloned.1.call-done = f32[24,2304]{1,0:T(8,128)} async-done(((f32[768,2304]{1,0:T(8,128)}), f32[24,2304]{1,0:T(8,128)}) %reduce-scatter.16.cloned.1.call-update) | async-done | bytes 221200
  668.7 142.2 %reduce-scatter.14.cloned.1.call-done = f32[96,768]{1,0:T(8,128)} async-done(((f32[3072,768]{1,0:T(8,128)}), f32[96,768]{1,0:T(8,128)}) %reduce-scatter.14.cloned.1.call-update) | async-done | bytes 294928 | tf_op jit(solution)/shard_map/reduce_scatter | solution.py:290
  810.9 141.2 %reduce-scatter.12.cloned.1.call-done = f32[24,3072]{1,0:T(8,128)} async-done(((f32[768,3072]{1,0:T(8,128)}), f32[24,3072]{1,0:T(8,128)}) %reduce-scatter.12.cloned.1.call-update) | async-done | bytes 294928 | tf_op jit(solution)/shard_map/reduce_scatter | solution.py:288
  (221 shorter events, 35.6 us)
Async XLA Ops:
  7.2 59.3 %copy-start.34 = (bf16[24,128]{1,0:T(8,128)(2,1)S(1)}, bf16[24,128]{1,0:T(8,128)(2,1)}, u32[]{:S(2)}) copy-start(bf16[24,128]{1,0:T(8,128)(2,1)} %param.40) | copy-start | bytes 18436
  7.2 132.7 %copy-start.16 = (bf16[1024,768]{1,0:T(8,128)(2,1)S(1)}, bf16[1024,768]{1,0:T(8,128)(2,1)}, u32[]{:S(2)}) copy-start(bf16[1024,768]{1,0:T(8,128)(2,1)} %param.24) | copy-start | bytes 4718596
  7.2 134.3 %all-gather.5.cloned.1.call-start = ((), (), s32[]{:S(2)}) async-start(), calls=%async_computation.5 | async-start | bytes 3649536 | tf_op jit(solution)/shard_map/all_gather | solution.py:129
  7.9 133.6 %copy-start.17 = (bf16[1024,768]{1,0:T(8,128)(2,1)S(1)}, bf16[1024,768]{1,0:T(8,128)(2,1)}, u32[]{:S(2)}) copy-start(bf16[1024,768]{1,0:T(8,128)(2,1)} %param.23) | copy-start | bytes 4718596
  8.0 190.8 %all-gather.7.cloned.1.call-start = ((), (), s32[]{:S(2)}) async-start(), calls=%async_computation.6 | async-start | bytes 1216512 | tf_op jit(solution)/shard_map/all_gather | solution.py:132
  8.7 196.1 %all-gather.9.cloned.1.call-start = ((), (), s32[]{:S(2)}) async-start(), calls=%async_computation.7 | async-start | bytes 4866048 | tf_op jit(solution)/shard_map/all_gather | solution.py:136
  9.4 250.7 %all-gather.11.cloned.1.call-start = ((), (), s32[]{:S(2)}) async-start(), calls=%async_computation.8 | async-start | bytes 4866048 | tf_op jit(solution)/shard_map/all_gather | solution.py:138
  10.0 548.5 %reduce-scatter.18.cloned.1.call-start = ((), (), s32[]{:S(2)}) async-start(), calls=%async_computation.13 | async-start | bytes 405504
  62.1 87.0 %copy-start.43 = (bf16[128]{0:T(256)(128)(2,1)}, bf16[128]{0:T(256)(128)(2,1)S(1)}, u32[]{:S(2)}) copy-start(bf16[128]{0:T(256)(128)(2,1)S(1)} %get-tuple-element.283) | copy-start | bytes 772
  64.6 317.8 %copy-start.28 = (f32[768]{0:T(1024)}, f32[768]{0:T(1024)S(1)}, u32[]{:S(2)}) copy-start(f32[768]{0:T(1024)S(1)} %convert_element_type.110) | copy-start | bytes 9220
  64.7 195.5 %copy-start.39 = (f32[768]{0:T(1024)}, f32[768]{0:T(1024)S(1)}, u32[]{:S(2)}) copy-start(f32[768]{0:T(1024)S(1)} %convert_element_type.111) | copy-start | bytes 9220
  193.0 9.7 %copy-start = (bf16[2,512,12,64]{1,3,2,0:T(8,128)(2,1)}, bf16[2,512,12,64]{1,3,2,0:T(8,128)(2,1)S(1)}, u32[]{:S(2)}) copy-start(bf16[2,512,12,64]{1,3,2,0:T(8,128)(2,1)S(1)} %get-tuple-element.474) | copy-start | bytes 4718596
  193.0 9.7 %copy-start.3 = (bf16[2,512,12,64]{1,3,2,0:T(8,128)(2,1)}, bf16[2,512,12,64]{1,3,2,0:T(8,128)(2,1)S(1)}, u32[]{:S(2)}) copy-start(bf16[2,512,12,64]{1,3,2,0:T(8,128)(2,1)S(1)} %get-tuple-element.485) | copy-start | bytes 4718596
  193.0 9.7 %copy-start.19 = (f32[2,12,512,1]{2,1,3,0:T(8,128)}, f32[2,12,512,1]{2,1,3,0:T(8,128)S(1)}, u32[]{:S(2)}) copy-start(f32[2,12,512,1]{2,1,3,0:T(8,128)S(1)} %get-tuple-element.443) | copy-start | bytes 147460
  202.7 1.7 copy-start.9
  202.7 179.7 %copy-start.21 = (f32[1024]{0:T(1024)}, f32[1024]{0:T(1024)S(1)}, u32[]{:S(2)}) copy-start(f32[1024]{0:T(1024)S(1)} %broadcast_multiply_fusion.5) | copy-start | bytes 12292
  204.8 177.7 %copy-start.30 = (f32[1024]{0:T(1024)}, f32[1024]{0:T(1024)S(1)}, u32[]{:S(2)}) copy-start(f32[1024]{0:T(1024)S(1)} %add_rsqrt_fusion.1) | copy-start | bytes 12292
  204.8 55.4 %copy-start.41 = (f32[768]{0:T(1024)S(1)}, f32[768]{0:T(1024)}, u32[]{:S(2)}) copy-start(f32[768]{0:T(1024)} %convert_element_type.115) | copy-start | bytes 9220
  260.2 10.3 %copy-start.23 = (f32[768]{0:T(1024)S(1)}, f32[768]{0:T(1024)}, u32[]{:S(2)}) copy-start(f32[768]{0:T(1024)} %convert_element_type.116) | copy-start | bytes 9220
  260.2 10.3 %copy-start.32 = (f32[768]{0:T(1024)S(1)}, f32[768]{0:T(1024)}, u32[]{:S(2)}) copy-start(f32[768]{0:T(1024)} %convert_element_type.117) | copy-start | bytes 9220
  270.1 2.2 copy-start.18
  270.5 4.6 copy-start.44
  270.5 5.4 copy-start.45
  270.5 68.2 %copy-start.42 = (f32[128]{0:T(128)S(1)}, f32[128]{0:T(128)}, u32[]{:S(2)}) copy-start(f32[128]{0:T(128)} %convert_element_type.120) | copy-start | bytes 1540
  274.2 0.8 copy-start.12
  338.7 8.0 copy-start.24
  346.7 211.8 %reduce-scatter.10.cloned.1.call-start = ((), (), s32[]{:S(2)}) async-start(), calls=%async_computation.9 | async-start | bytes 2433024 | tf_op jit(solution)/shard_map/reduce_scatter | solution.py:284
  352.0 19.7 %copy-start.10 = (f32[1024,768]{0,1:T(8,128)S(1)}, f32[1024,768]{0,1:T(8,128)}, u32[]{:S(2)}) copy-start(f32[1024,768]{0,1:T(8,128)} %copy-done.9) | copy-start | bytes 9437188
  382.5 3.4 copy-start.46
  384.2 1.6 copy-start.14
  390.9 5.5 copy-start.1
  390.9 5.5 copy-start.4
  390.9 5.5 copy-start.20
  396.4 272.3 %reduce-scatter.16.cloned.1.call-start = ((), (), s32[]{:S(2)}) async-start(), calls=%async_computation.12 | async-start | bytes 7299072
  396.5 2.1 copy-start.6
  396.5 2.1 copy-start.7
  413.7 2.0 copy-start.8
  421.7 3.4 copy-start.2
  421.7 3.4 copy-start.5
  425.1 2.1 copy-start.6
  425.1 2.1 copy-start.7
  442.3 2.0 copy-start.8
  450.3 3.4 copy-start.2
  450.3 3.4 copy-start.5
  471.8 1.9 copy-start.15
  471.8 339.1 %reduce-scatter.14.cloned.1.call-start = ((), (), s32[]{:S(2)}) async-start(), calls=%async_computation.11 | async-start | bytes 9732096 | tf_op jit(solution)/shard_map/reduce_scatter | solution.py:290
  484.0 1.9 copy-start.11
  484.0 1.9 copy-start.22
  484.0 1.9 copy-start.29
  484.0 1.9 copy-start.31
  484.0 1.9 copy-start.40
  484.0 468.1 %reduce-scatter.12.cloned.1.call-start = ((), (), s32[]{:S(2)}) async-start(), calls=%async_computation.10 | async-start | bytes 9732096 | tf_op jit(solution)/shard_map/reduce_scatter | solution.py:288
  496.3 2.8 copy-start.25
  496.3 2.8 copy-start.13
  496.4 6.2 copy-start.26
  496.4 6.2 copy-start.27
  496.4 6.2 copy-start.33
  496.4 6.2 copy-start.35
  496.4 6.2 copy-start.36
  496.4 6.2 copy-start.37
  496.4 6.2 copy-start.38
Sparse Core Ops, SparseCore 0:
  10.8 63.2 all-gather.4
  76.9 52.7 all-gather.6
  132.5 62.5 all-gather.8
  197.8 62.3 all-gather.10
  346.8 92.6 reduce-scatter.17
  446.0 98.1 reduce-scatter.9
  550.5 118.1 reduce-scatter.15
  676.2 134.7 reduce-scatter.13
  817.4 134.6 reduce-scatter.11
